TPU v7x, 32 devices: a whole 2x2x4 slice. The times are simulated.
32 devices in a mesh: groups: 2 (over x), gx: 8 (over z, y), shot: 2 (over core).
Axes of the slice: x: 2, y: 2, z: 4, core: 2. Of those that a mesh axis runs over, the one named last changes fastest.
Arguments:
- src_now: float32 [8, 128, 64, 128], P(('groups', 'shot'), 'gx'), parts along dimension 0, may hold values from -6 to 6
- src_prev: float32 [8, 128, 64, 128], P(('groups', 'shot'), 'gx'), parts along dimension 0, may hold values from -6 to 6
- rec_now: float32 [8, 128, 64, 128], P(('groups', 'shot'), 'gx'), parts along dimension 0, may hold values from -6 to 6
- rec_prev: float32 [8, 128, 64, 128], P(('groups', 'shot'), 'gx'), parts along dimension 0, may hold values from -6 to 6
- courant_sq: float32 [256, 64, 128], P(('groups', 'gx')), parts along dimension 0, may hold values from 0.05 to 0.3
- wavelet: float32 [8, 4], P(('groups', 'shot')), parts along dimension 0, may hold values from -8 to 8
- traces: float32 [8, 4, 128], P(('groups', 'shot'), None, 'gx'), parts along dimension 0, may hold values from -6 to 6
- positions: int32 [8, 4], P(('groups', 'shot')), parts along dimension 0, may hold values from 0 to 127, as said below
Outputs:
- angle_image: float32 [16, 128, 32, 128], P(('groups', 'shot'), 'gx'), parts along dimension 0
There are 2 independent parts, one for each index of `groups`. A program takes and returns all parts, laid end to end along the dimension named above; each array names one. Nothing has to cross between parts.
Inputs may be any that keep to these rules, and one draw needn't show every extreme that they name: `positions`: column 0 lies in 0 .. 127, columns 1 and 3 in 0 .. 127, column 2 in 0 .. 63; one shot of each patch has its source at x 128 - 1, y * 128 - 1, depth 64 - 1 and its receiver line at y 0.
All inputs are finite; a program needn't handle non-finite values.
Results may differ from a plain program's by a relative error of at most 0.0001.
Values sent between devices are 32-bit elements; how exact they have to be, the bound alone decides.
A program may use at most 192 MiB of HBM per device.

v0:
```python
import functools
import math

import jax
import jax.numpy as jnp
from jax import lax
from jax.experimental import pallas as pl
from jax.experimental.pallas import tpu as pltpu
from jax.sharding import PartitionSpec as P

STEPS = 4
IMAGES = 2
LAGS = 49
ANGLES = 8
HALF = (LAGS - 1) // 2
MESH = pl.DeviceIdType.MESH


def kernel(
    n,
    scale,
    rows,
    positions,
    wavelet,
    traces,
    src_now,
    src_prev,
    rec_now,
    rec_prev,
    courant_hbm,
    out,
    level,
    courant,
    window,
    image,
    from_core,
    summed,
    from_pair,
    product,
    load_sem,
    halo_send,
    halo_recv,
    pair_send,
    pair_recv,
    up_send,
    up_recv,
    down_send,
    down_recv,
    core_send,
    core_recv,
    out_send,
    out_recv,
):
    planes, depth, width = courant.shape
    block = planes // 2
    shots = src_now.shape[0]
    angles_out, _, depth_out, _ = out.shape
    me = lax.axis_index("gx")
    core = lax.axis_index("shot")
    y = lax.rem(me, 2)
    pair = me + 1 - 2 * y
    other = 1 - core
    has_below = me >= 2
    has_above = me < n - 2

    loads = []
    for i, (ref, k, f) in enumerate(
        ((src_now, 1, 0), (rec_now, 1, 1), (src_prev, 0, 0), (rec_prev, 0, 1))
    ):
        loads.append(
            pltpu.make_async_copy(ref, level.at[k, f, :, pl.ds(1, planes)], load_sem.at[i])
        )
    loads.append(pltpu.make_async_copy(courant_hbm, courant, load_sem.at[4]))
    for load in loads:
        load.start()

    barrier = pltpu.get_barrier_semaphore()
    for step in (-2, -1, 1, 2):
        there = me + step

        @pl.when((there >= 0) & (there < n))
        def _():
            pl.semaphore_signal(barrier, inc=1, device_id={"gx": there}, device_id_type=MESH)

    pl.semaphore_signal(barrier, inc=1, device_id={"shot": other}, device_id_type=MESH)

    edge = jnp.zeros((rows, width), jnp.float32)
    full = jnp.zeros((depth, width), jnp.float32)

    @pl.when(me == 0)
    def _():
        for k in range(1, STEPS + 1):
            for f in range(2):
                for s in range(shots):
                    level[k, f, s, 0] = full

    @pl.when(me == n - 1)
    def _():
        for k in range(1, STEPS + 1):
            for f in range(2):
                for s in range(shots):
                    level[k, f, s, planes + 1] = full

    @pl.when(jnp.logical_not(has_below))
    def _():
        @pl.loop(0, HALF)
        def _(q):
            for g in range(IMAGES):
                for f in range(2):
                    window[g, f, q] = edge

    @pl.when(jnp.logical_not(has_above))
    def _():
        @pl.loop(0, HALF)
        def _(q):
            for g in range(IMAGES):
                for f in range(2):
                    window[g, f, HALF + 2 * planes + q] = edge

    peers = jnp.minimum(me, 2) + jnp.minimum(n - 1 - me, 2) + 1
    pl.semaphore_wait(barrier, peers)

    def halo(t, side):
        height = depth if t == 0 else rows
        kept = pl.ds(0, height)
        source, target = (planes, 0) if side == 0 else (1, planes + 1)
        return pltpu.make_async_remote_copy(
            src_ref=level.at[1 + t, :, :, source, kept],
            dst_ref=level.at[1 + t, :, :, target, kept],
            send_sem=halo_send.at[t, side],
            recv_sem=halo_recv.at[t, side],
            device_id={"gx": me + 1 if side == 0 else me - 1},
            device_id_type=MESH,
        )

    def send_halo(t):
        @pl.when(me < n - 1)
        def _():
            halo(t, 0).start()

        @pl.when(me > 0)
        def _():
            halo(t, 1).start()

    def wait_halo(t):
        @pl.when(me > 0)
        def _():
            halo(t, 0).wait_recv()

        @pl.when(me < n - 1)
        def _():
            halo(t, 1).wait_recv()

    z_row = lax.broadcasted_iota(jnp.int32, (rows, width), 0)
    y_lane = lax.broadcasted_iota(jnp.int32, (rows, width), 1)
    first = me * planes

    def plane_step(t, x):
        speed = courant[x - 1, :rows]
        tall = depth if t == 0 else rows
        for s in range(shots):
            for f in range(2):
                now_tall = level[1 + t, f, s, x, :tall]
                now = now_tall[:rows]
                low = level[1 + t, f, s, x - 1, :rows]
                high = level[1 + t, f, s, x + 1, :rows]
                zeros = jnp.zeros((1, width), jnp.float32)
                deeper = jnp.concatenate([now_tall[1:], zeros], axis=0)[:rows]
                shallower = jnp.concatenate([zeros, now[: rows - 1]], axis=0)
                left = jnp.where(y_lane == 0, 0.0, pltpu.roll(now, 1, 1))
                right = jnp.where(y_lane == width - 1, 0.0, pltpu.roll(now, width - 1, 1))
                beside = low + high + deeper + shallower + left + right
                nxt = 2.0 * now - level[t, f, s, x, :rows] + speed * (beside - 6.0 * now)
                if f == 0:
                    amount = jnp.where(first + x - 1 == positions[s, 0], wavelet[s, t], 0.0)
                    hit = (z_row == positions[s, 2]) & (y_lane == positions[s, 1])
                else:
                    amount = traces[s, STEPS - 1 - t, x - 1]
                    hit = (z_row == 0) & (y_lane == positions[s, 3])
                level[2 + t, f, s, x, :rows] = nxt + jnp.where(hit, amount, 0.0)

    def wave_step(t):
        @pl.loop(2, planes)
        def _(x):
            plane_step(t, x)

        wait_halo(t)
        for half in range(2):
            @pl.loop(0, 1)
            def _(_i, half=half):
                plane_step(t, 1 + half * (planes - 1))

    def pair_copy(g, part):
        at = block * (1 - y) if part == 0 else block * y
        return pltpu.make_async_remote_copy(
            src_ref=level.at[2 * g + 3, :, 1 - y, pl.ds(1 + at, block), pl.ds(0, rows)],
            dst_ref=window.at[g, :, pl.ds(HALF + planes * y + at, block)],
            send_sem=pair_send.at[g, part],
            recv_sem=pair_recv.at[g, part],
            device_id={"gx": pair},
            device_id_type=MESH,
        )

    def up_copy(g, k):
        return pltpu.make_async_remote_copy(
            src_ref=window.at[g, :, pl.ds(HALF + block * (k + 1), block)],
            dst_ref=window.at[g, :, pl.ds(block * k, block)],
            send_sem=up_send.at[g, k],
            recv_sem=up_recv.at[g, k],
            device_id={"gx": me + 2},
            device_id_type=MESH,
        )

    def down_copy(g, k):
        return pltpu.make_async_remote_copy(
            src_ref=window.at[g, :, pl.ds(HALF + block * k, block)],
            dst_ref=window.at[g, :, pl.ds(HALF + 2 * planes + block * k, block)],
            send_sem=down_send.at[g, k],
            recv_sem=down_recv.at[g, k],
            device_id={"gx": me - 2},
            device_id_type=MESH,
        )

    def send_inner(g, owner):
        @pl.when(has_above)
        def _():
            up_copy(g, owner).start()

        @pl.when(has_below)
        def _():
            down_copy(g, 1 + owner).start()

    def send_outer(g, owner):
        @pl.when(has_above & (owner == 1))
        def _():
            up_copy(g, 2).start()

        @pl.when(has_below & (owner == 0))
        def _():
            down_copy(g, 0).start()

    def own_out(g):
        pair_copy(g, 0).start()
        pair_copy(g, 1).start()

        @pl.loop(0, planes)
        def _(x):
            for f in range(2):
                window[g, f, HALF + planes * y + x] = level[2 * g + 3, f, y, 1 + x, :rows]

        send_inner(g, y)
        send_outer(g, y)

    def relay(g):
        pair_copy(g, 0).wait_recv()
        send_inner(g, 1 - y)
        pair_copy(g, 1).wait_recv()
        send_outer(g, 1 - y)

    def wait_window(g):
        for k in range(3):
            @pl.when(has_below)
            def _():
                up_copy(g, k).wait_recv()

            @pl.when(has_above)
            def _():
                down_copy(g, k).wait_recv()

    def image_chunk(g, chunk):
        @pl.loop(0, block)
        def _(x):
            at = HALF + chunk * block + x
            totals = [None] * ANGLES
            for h in range(HALF + 1):
                reach = depth_out + (ANGLES - 1) * h // ANGLES
                tall = min(rows, -(-reach // 8) * 8)
                value = window[g, 0, at - h, :tall] * window[g, 1, at + h, :tall]
                if h:
                    value = value + window[g, 0, at + h, :tall] * window[g, 1, at - h, :tall]
                if h > 1:
                    product[h % 4, :tall] = value
                for a in range(ANGLES):
                    moved = a * h // ANGLES
                    piece = product[h % 4, moved : moved + depth_out] if moved else value[:depth_out]
                    totals[a] = piece if totals[a] is None else totals[a] + piece
            for a in range(ANGLES):
                if g:
                    totals[a] = totals[a] + image[chunk, a, x]
                image[chunk, a, x] = totals[a]

    def core_copy(chunk):
        return pltpu.make_async_remote_copy(
            src_ref=image.at[chunk, pl.ds(angles_out * other, angles_out)],
            dst_ref=from_core.at[chunk],
            send_sem=core_send.at[chunk],
            recv_sem=core_recv.at[chunk],
            device_id={"shot": other},
            device_id_type=MESH,
        )

    def out_copy(j):
        return pltpu.make_async_remote_copy(
            src_ref=summed.at[j],
            dst_ref=from_pair.at[j],
            send_sem=out_send.at[j],
            recv_sem=out_recv.at[j],
            device_id={"gx": pair},
            device_id_type=MESH,
        )

    def pass_on(j):
        chunk = 2 * (1 - y) + j
        core_copy(chunk).wait_recv()

        @pl.loop(0, block)
        def _(x):
            for a in range(angles_out):
                summed[j, a, x] = image[chunk, angles_out * core + a, x] + from_core[chunk, a, x]

        out_copy(j).start()

    def finish(j):
        chunk = 2 * y + j
        core_copy(chunk).wait_recv()
        out_copy(j).wait_recv()

        @pl.loop(0, block)
        def _(x):
            for a in range(angles_out):
                value = image[chunk, angles_out * core + a, x] + from_core[chunk, a, x]
                out[a, j * block + x] = (value + from_pair[j, a, x]) * scale

    loads[0].wait()
    loads[1].wait()
    send_halo(0)
    for load in loads[2:]:
        load.wait()
    wave_step(0)
    send_halo(1)
    wave_step(1)
    send_halo(2)
    own_out(0)
    wave_step(2)
    send_halo(3)
    relay(0)
    wave_step(3)
    own_out(1)
    wait_window(0)

    @pl.loop(0, 4)
    def _(chunk):
        image_chunk(0, chunk)

    relay(1)
    wait_window(1)
    for j in range(2):
        image_chunk(1, 2 * (1 - y) + j)
        core_copy(2 * (1 - y) + j).start()
        if j:
            pass_on(0)
    for j in range(2):
        image_chunk(1, 2 * y + j)
        core_copy(2 * y + j).start()
        if j == 0:
            pass_on(1)
    for j in range(2):
        finish(j)

    for t in range(STEPS):
        @pl.when(me < n - 1)
        def _():
            halo(t, 0).wait_send()

        @pl.when(me > 0)
        def _():
            halo(t, 1).wait_send()

    for g in range(IMAGES):
        for part in range(2):
            pair_copy(g, part).wait_send()
        for k in range(3):
            @pl.when(has_above)
            def _():
                up_copy(g, k).wait_send()

            @pl.when(has_below)
            def _():
                down_copy(g, k).wait_send()

    for chunk in range(4):
        core_copy(chunk).wait_send()
    for j in range(2):
        out_copy(j).wait_send()


def solution(mesh):
    n = mesh.shape["gx"]
    cores = mesh.shape["shot"]

    def local(src_now, src_prev, rec_now, rec_prev, courant_sq, wavelet, traces, positions):
        shots, planes, depth, width = src_now.shape
        depth_out = depth // 2
        reach = depth_out + (ANGLES - 1) * HALF // ANGLES
        rows = min(depth, -(-(reach + STEPS - 1) // 8) * 8)
        block = planes // 2
        assert n % 2 == 0 and cores == 2 and shots == 2 and 3 * block == HALF
        angles_out = ANGLES // cores
        scale = 1.0 / math.sqrt(LAGS * shots * cores * IMAGES)
        vmem = pl.BlockSpec(memory_space=pltpu.VMEM)
        smem = pl.BlockSpec(memory_space=pltpu.SMEM)
        hbm = pl.BlockSpec(memory_space=pl.ANY)
        f32 = jnp.float32
        dma = pltpu.SemaphoreType.DMA
        return pl.pallas_call(
            functools.partial(kernel, n, scale, rows),
            out_shape=jax.ShapeDtypeStruct((angles_out, planes, depth_out, width), f32),
            in_specs=[smem] * 3 + [hbm] * 5,
            out_specs=vmem,
            scratch_shapes=[
                pltpu.VMEM((STEPS + 2, 2, shots, planes + 2, depth, width), f32),
                pltpu.VMEM((planes, depth, width), f32),
                pltpu.VMEM((IMAGES, 2, 2 * planes + 2 * HALF, rows, width), f32),
                pltpu.VMEM((4, ANGLES, block, depth_out, width), f32),
                pltpu.VMEM((4, angles_out, block, depth_out, width), f32),
                pltpu.VMEM((2, angles_out, block, depth_out, width), f32),
                pltpu.VMEM((2, angles_out, block, depth_out, width), f32),
                pltpu.VMEM((4, rows, width), f32),
                dma((5,)),
                dma((STEPS, 2)),
                dma((STEPS, 2)),
                dma((IMAGES, 2)),
                dma((IMAGES, 2)),
                dma((IMAGES, 3)),
                dma((IMAGES, 3)),
                dma((IMAGES, 3)),
                dma((IMAGES, 3)),
                dma((4,)),
                dma((4,)),
                dma((2,)),
                dma((2,)),
            ],
            compiler_params=pltpu.CompilerParams(
                collective_id=0, has_side_effects=True, vmem_limit_bytes=60 * 1024 * 1024
            ),
        )(positions, wavelet, traces, src_now, src_prev, rec_now, rec_prev, courant_sq)

    placed = (
        P(("groups", "shot"), "gx", None, None),
        P(("groups", "shot"), "gx", None, None),
        P(("groups", "shot"), "gx", None, None),
        P(("groups", "shot"), "gx", None, None),
        P(("groups", "gx"), None, None),
        P(("groups", "shot"), None),
        P(("groups", "shot"), None, "gx"),
        P(("groups", "shot"), None),
    )
    return jax.shard_map(
        local,
        mesh=mesh,
        in_specs=placed,
        out_specs=P(("groups", "shot"), "gx", None, None),
        check_vma=False,
    )
```

profile of v0, /device:TPU:0, one launch (start us, length us, event | category | flops | bytes accessed | tf_op | source)
XLA Modules:
  0.0 121.7 jit_solution(56419251311597735)
XLA Ops:
  0.0 119.4 %shard_map.82 = f32[4,16,32,128]{3,2,1,0:T(8,128)} custom-call(s32[2,4]{1,0:T(2,128)} %positions.1, f32[2,4]{1,0:T(2,128)} %wavelet.1, f32[2,4,16]{2,1,0:T(4,128)} %traces.1, f32[2,16,64,128]{3,2,1,0:T(8,128)} %src_now.1, f32[2,16,64,128]{3,2,1,0:T(8,128)} %src_prev.1, f32[2,16,64,128]{3,2,1,0:T(8,128)} %rec_now.1, f32[2,16,64,128]{3,2,1,0:T(8,128)} %rec_prev.1, ...), custom_call_target="tpu_custom_call" | custom-call | tf_op jit(solution)/shard_map/pallas_call | solution.py:415
  119.5 2.3 %copy.10 = f32[4,16,32,128]{3,2,1,0:T(8,128)} copy(f32[4,16,32,128]{3,2,1,0:T(8,128)} %shard_map.82) | data formatting | bytes 2097152
where the time goes:
time: 122 us
  Pallas kernels  119 us (98%)
  local copies, waits for them, and re-layouts  2.26 us (2%)
    pallas_call x1, Pallas kernels, local(): pl.pallas_call(functools.partial(kernel, n, scale, rows), out_shape=jax.S...  119 us

commit v1 on v0

--- a/solution.py
+++ b/solution.py
@@ -20,6 +20,7 @@
     n,
     scale,
     rows,
+    sent,
     positions,
     wavelet,
     traces,
@@ -32,6 +33,7 @@
     level,
     courant,
     window,
+    outgoing,
     image,
     from_core,
     summed,
@@ -54,7 +56,9 @@
     planes, depth, width = courant.shape
     block = planes // 2
     shots = src_now.shape[0]
-    angles_out, _, depth_out, _ = out.shape
+    depth_out = out.shape[2]
+    packs = from_core.shape[1]
+    lanes = width // 2
     me = lax.axis_index("gx")
     core = lax.axis_index("shot")
     y = lax.rem(me, 2)
@@ -121,7 +125,7 @@
     pl.semaphore_wait(barrier, peers)
 
     def halo(t, side):
-        height = depth if t == 0 else rows
+        height = min(depth, rows + 1) if t == 0 else rows
         kept = pl.ds(0, height)
         source, target = (planes, 0) if side == 0 else (1, planes + 1)
         return pltpu.make_async_remote_copy(
@@ -193,8 +197,8 @@
     def pair_copy(g, part):
         at = block * (1 - y) if part == 0 else block * y
         return pltpu.make_async_remote_copy(
-            src_ref=level.at[2 * g + 3, :, 1 - y, pl.ds(1 + at, block), pl.ds(0, rows)],
-            dst_ref=window.at[g, :, pl.ds(HALF + planes * y + at, block)],
+            src_ref=outgoing.at[g, :, pl.ds(at, block), pl.ds(0, sent)],
+            dst_ref=window.at[g, :, pl.ds(HALF + planes * y + at, block), pl.ds(0, sent)],
             send_sem=pair_send.at[g, part],
             recv_sem=pair_recv.at[g, part],
             device_id={"gx": pair},
@@ -203,8 +207,8 @@
 
     def up_copy(g, k):
         return pltpu.make_async_remote_copy(
-            src_ref=window.at[g, :, pl.ds(HALF + block * (k + 1), block)],
-            dst_ref=window.at[g, :, pl.ds(block * k, block)],
+            src_ref=window.at[g, :, pl.ds(HALF + block * (k + 1), block), pl.ds(0, sent)],
+            dst_ref=window.at[g, :, pl.ds(block * k, block), pl.ds(0, sent)],
             send_sem=up_send.at[g, k],
             recv_sem=up_recv.at[g, k],
             device_id={"gx": me + 2},
@@ -213,8 +217,8 @@
 
     def down_copy(g, k):
         return pltpu.make_async_remote_copy(
-            src_ref=window.at[g, :, pl.ds(HALF + block * k, block)],
-            dst_ref=window.at[g, :, pl.ds(HALF + 2 * planes + block * k, block)],
+            src_ref=window.at[g, :, pl.ds(HALF + block * k, block), pl.ds(0, sent)],
+            dst_ref=window.at[g, :, pl.ds(HALF + 2 * planes + block * k, block), pl.ds(0, sent)],
             send_sem=down_send.at[g, k],
             recv_sem=down_recv.at[g, k],
             device_id={"gx": me - 2},
@@ -239,15 +243,23 @@
         def _():
             down_copy(g, 0).start()
 
+    first_half = y_lane < lanes
+
     def own_out(g):
-        pair_copy(g, 0).start()
-        pair_copy(g, 1).start()
-
         @pl.loop(0, planes)
         def _(x):
             for f in range(2):
-                window[g, f, HALF + planes * y + x] = level[2 * g + 3, f, y, 1 + x, :rows]
-
+                one = level[2 * g + 3, f, 0, 1 + x, :rows]
+                two = level[2 * g + 3, f, 1, 1 + x, :rows]
+                halves = (
+                    jnp.where(first_half, one, pltpu.roll(two, lanes, 1)),
+                    jnp.where(first_half, pltpu.roll(one, lanes, 1), two),
+                )
+                window[g, f, HALF + planes * y + x] = jnp.where(y == 0, halves[0], halves[1])
+                outgoing[g, f, x] = jnp.where(y == 0, halves[1], halves[0])
+
+        pair_copy(g, 0).start()
+        pair_copy(g, 1).start()
         send_inner(g, y)
         send_outer(g, y)
 
@@ -284,14 +296,18 @@
                     moved = a * h // ANGLES
                     piece = product[h % 4, moved : moved + depth_out] if moved else value[:depth_out]
                     totals[a] = piece if totals[a] is None else totals[a] + piece
-            for a in range(ANGLES):
+            for i in range(ANGLES // 2):
+                even, odd = totals[2 * i], totals[2 * i + 1]
+                low = first_half[:depth_out]
+                folded = jnp.where(low, even, odd)
+                folded = folded + pltpu.roll(jnp.where(low, odd, even), lanes, 1)
                 if g:
-                    totals[a] = totals[a] + image[chunk, a, x]
-                image[chunk, a, x] = totals[a]
+                    folded = folded + image[chunk, i, x]
+                image[chunk, i, x] = folded
 
     def core_copy(chunk):
         return pltpu.make_async_remote_copy(
-            src_ref=image.at[chunk, pl.ds(angles_out * other, angles_out)],
+            src_ref=image.at[chunk, pl.ds(packs * other, packs)],
             dst_ref=from_core.at[chunk],
             send_sem=core_send.at[chunk],
             recv_sem=core_recv.at[chunk],
@@ -315,8 +331,8 @@
 
         @pl.loop(0, block)
         def _(x):
-            for a in range(angles_out):
-                summed[j, a, x] = image[chunk, angles_out * core + a, x] + from_core[chunk, a, x]
+            for i in range(packs):
+                summed[j, i, x] = image[chunk, packs * core + i, x] + from_core[chunk, i, x]
 
         out_copy(j).start()
 
@@ -327,9 +343,14 @@
 
         @pl.loop(0, block)
         def _(x):
-            for a in range(angles_out):
-                value = image[chunk, angles_out * core + a, x] + from_core[chunk, a, x]
-                out[a, j * block + x] = (value + from_pair[j, a, x]) * scale
+            low = first_half[:depth_out]
+            for i in range(packs):
+                mine = image[chunk, packs * core + i, x] + from_core[chunk, i, x]
+                theirs = from_pair[j, i, x]
+                left = jnp.where(y == 0, mine, theirs) * scale
+                right = jnp.where(y == 0, theirs, mine) * scale
+                out[2 * i, j * block + x] = jnp.where(low, left, pltpu.roll(right, lanes, 1))
+                out[2 * i + 1, j * block + x] = jnp.where(low, pltpu.roll(left, lanes, 1), right)
 
     loads[0].wait()
     loads[1].wait()
@@ -404,7 +425,7 @@
         reach = depth_out + (ANGLES - 1) * HALF // ANGLES
         rows = min(depth, -(-(reach + STEPS - 1) // 8) * 8)
         block = planes // 2
-        assert n % 2 == 0 and cores == 2 and shots == 2 and 3 * block == HALF
+        assert n % 2 == 0 and cores == 2 and shots == 2 and 3 * block == HALF and width % 2 == 0
         angles_out = ANGLES // cores
         scale = 1.0 / math.sqrt(LAGS * shots * cores * IMAGES)
         vmem = pl.BlockSpec(memory_space=pltpu.VMEM)
@@ -413,7 +434,7 @@
         f32 = jnp.float32
         dma = pltpu.SemaphoreType.DMA
         return pl.pallas_call(
-            functools.partial(kernel, n, scale, rows),
+            functools.partial(kernel, n, scale, rows, reach),
             out_shape=jax.ShapeDtypeStruct((angles_out, planes, depth_out, width), f32),
             in_specs=[smem] * 3 + [hbm] * 5,
             out_specs=vmem,
@@ -421,10 +442,11 @@
                 pltpu.VMEM((STEPS + 2, 2, shots, planes + 2, depth, width), f32),
                 pltpu.VMEM((planes, depth, width), f32),
                 pltpu.VMEM((IMAGES, 2, 2 * planes + 2 * HALF, rows, width), f32),
-                pltpu.VMEM((4, ANGLES, block, depth_out, width), f32),
-                pltpu.VMEM((4, angles_out, block, depth_out, width), f32),
-                pltpu.VMEM((2, angles_out, block, depth_out, width), f32),
-                pltpu.VMEM((2, angles_out, block, depth_out, width), f32),
+                pltpu.VMEM((IMAGES, 2, planes, rows, width), f32),
+                pltpu.VMEM((4, ANGLES // 2, block, depth_out, width), f32),
+                pltpu.VMEM((4, angles_out // 2, block, depth_out, width), f32),
+                pltpu.VMEM((2, angles_out // 2, block, depth_out, width), f32),
+                pltpu.VMEM((2, angles_out // 2, block, depth_out, width), f32),
                 pltpu.VMEM((4, rows, width), f32),
                 dma((5,)),
                 dma((STEPS, 2)),

time: 122 us -> 112 us (0.918)
  Pallas kernels: 119 us -> 110 us
    pallas_call x1, Pallas kernels: 119 us -> 110 us  [local(): pl.pallas_call(functools.partial(kernel, n, scale, rows, reach), out_shap...]
where the time goes in v1:
time: 112 us
  Pallas kernels  110 us (98%)
  local copies, waits for them, and re-layouts  2.26 us (2%)
    pallas_call x1, Pallas kernels, local(): pl.pallas_call(functools.partial(kernel, n, scale, rows, reach), out_shap...  110 us
    unnamed x1, local copies, waits for them, and re-layouts  2.26 us

profile of v1, /device:TPU:0, one launch (start us, length us, event | category | flops | bytes accessed | tf_op | source)
XLA Modules:
  0.0 111.8 jit_solution(14106339725322213058)
XLA Ops:
  0.0 109.6 %shard_map.82 = f32[4,16,32,128]{3,2,1,0:T(8,128)} custom-call(s32[2,4]{1,0:T(2,128)} %positions.1, f32[2,4]{1,0:T(2,128)} %wavelet.1, f32[2,4,16]{2,1,0:T(4,128)} %traces.1, f32[2,16,64,128]{3,2,1,0:T(8,128)} %src_now.1, f32[2,16,64,128]{3,2,1,0:T(8,128)} %src_prev.1, f32[2,16,64,128]{3,2,1,0:T(8,128)} %rec_now.1, f32[2,16,64,128]{3,2,1,0:T(8,128)} %rec_prev.1, ...), custom_call_target="tpu_custom_call" | custom-call | tf_op jit(solution)/shard_map/pallas_call | solution.py:436
  109.6 2.3 %copy.10 = f32[4,16,32,128]{3,2,1,0:T(8,128)} copy(f32[4,16,32,128]{3,2,1,0:T(8,128)} %shard_map.82) | data formatting | bytes 2097152

commit v2 on v1

--- a/solution.py
+++ b/solution.py
@@ -245,29 +245,44 @@
 
     first_half = y_lane < lanes
 
+    def order(g):
+        return (0, 1) if g == 0 else (1, 0)
+
     def own_out(g):
-        @pl.loop(0, planes)
-        def _(x):
-            for f in range(2):
-                one = level[2 * g + 3, f, 0, 1 + x, :rows]
-                two = level[2 * g + 3, f, 1, 1 + x, :rows]
-                halves = (
-                    jnp.where(first_half, one, pltpu.roll(two, lanes, 1)),
-                    jnp.where(first_half, pltpu.roll(one, lanes, 1), two),
-                )
-                window[g, f, HALF + planes * y + x] = jnp.where(y == 0, halves[0], halves[1])
-                outgoing[g, f, x] = jnp.where(y == 0, halves[1], halves[0])
-
-        pair_copy(g, 0).start()
-        pair_copy(g, 1).start()
-        send_inner(g, y)
-        send_outer(g, y)
+        for part in order(g):
+            at = block * (1 - y) if part == 0 else block * y
+
+            @pl.loop(0, block)
+            def _(i, at=at):
+                x = at + i
+                for f in range(2):
+                    one = level[2 * g + 3, f, 0, 1 + x, :rows]
+                    two = level[2 * g + 3, f, 1, 1 + x, :rows]
+                    halves = (
+                        jnp.where(first_half, one, pltpu.roll(two, lanes, 1)),
+                        jnp.where(first_half, pltpu.roll(one, lanes, 1), two),
+                    )
+                    window[g, f, HALF + planes * y + x] = jnp.where(y == 0, halves[0], halves[1])
+                    outgoing[g, f, x] = jnp.where(y == 0, halves[1], halves[0])
+
+            pair_copy(g, part).start()
+            (send_outer if part else send_inner)(g, y)
 
     def relay(g):
-        pair_copy(g, 0).wait_recv()
-        send_inner(g, 1 - y)
-        pair_copy(g, 1).wait_recv()
-        send_outer(g, 1 - y)
+        for part in order(g):
+            pair_copy(g, part).wait_recv()
+            (send_outer if part else send_inner)(g, 1 - y)
+
+    def wait_block(g, late, distance):
+        below = (y == 0) if late else (y == 1)
+
+        @pl.when(below & has_below)
+        def _():
+            up_copy(g, 2 - distance).wait_recv()
+
+        @pl.when(jnp.logical_not(below) & has_above)
+        def _():
+            down_copy(g, distance).wait_recv()
 
     def wait_window(g):
         for k in range(3):
@@ -279,12 +294,12 @@
             def _():
                 down_copy(g, k).wait_recv()
 
-    def image_chunk(g, chunk):
+    def image_chunk(g, chunk, lags):
         @pl.loop(0, block)
         def _(x):
             at = HALF + chunk * block + x
             totals = [None] * ANGLES
-            for h in range(HALF + 1):
+            for h in lags:
                 reach = depth_out + (ANGLES - 1) * h // ANGLES
                 tall = min(rows, -(-reach // 8) * 8)
                 value = window[g, 0, at - h, :tall] * window[g, 1, at + h, :tall]
@@ -325,8 +340,8 @@
             device_id_type=MESH,
         )
 
-    def pass_on(j):
-        chunk = 2 * (1 - y) + j
+    def pass_on(chunk):
+        j = chunk - 2 * (1 - y)
         core_copy(chunk).wait_recv()
 
         @pl.loop(0, block)
@@ -368,25 +383,39 @@
     wave_step(3)
     own_out(1)
     wait_window(0)
+    near, far = range(block + 1), range(2 * block + 1, HALF + 1)
 
     @pl.loop(0, 4)
     def _(chunk):
-        image_chunk(0, chunk)
+        image_chunk(0, chunk, range(HALF + 1))
 
     relay(1)
-    wait_window(1)
-    for j in range(2):
-        image_chunk(1, 2 * (1 - y) + j)
-        core_copy(2 * (1 - y) + j).start()
-        if j:
-            pass_on(0)
-    for j in range(2):
-        image_chunk(1, 2 * y + j)
-        core_copy(2 * y + j).start()
-        if j == 0:
-            pass_on(1)
-    for j in range(2):
-        finish(j)
+    chunks = [c + y * (3 - 2 * c) for c in range(4)]
+    wait_block(1, False, 0)
+    wait_block(1, False, 1)
+
+    @pl.loop(2, 4)
+    def _(c):
+        image_chunk(1, c + y * (3 - 2 * c), range(2 * block + 1))
+
+    wait_block(1, True, 0)
+    image_chunk(1, chunks[2], far)
+    core_copy(chunks[2]).start()
+    image_chunk(1, chunks[1], range(2 * block + 1))
+    pass_on(chunks[2])
+    image_chunk(1, chunks[0], near)
+    wait_block(1, False, 2)
+    image_chunk(1, chunks[3], far)
+    core_copy(chunks[3]).start()
+    wait_block(1, True, 1)
+    wait_block(1, True, 2)
+    image_chunk(1, chunks[1], far)
+    core_copy(chunks[1]).start()
+    pass_on(chunks[3])
+    image_chunk(1, chunks[0], range(block + 1, HALF + 1))
+    core_copy(chunks[0]).start()
+    finish(1 - y)
+    finish(y)
 
     for t in range(STEPS):
         @pl.when(me < n - 1)

time: 112 us -> 105 us (0.938)
  Pallas kernels: 110 us -> 102 us
    pallas_call x1, Pallas kernels: 110 us -> 102 us  [local(): pl.pallas_call(functools.partial(kernel, n, scale, rows, reach), out_shap...]
where the time goes in v2:
time: 105 us
  Pallas kernels  102 us (97%)
  local copies, waits for them, and re-layouts  2.26 us (2%)
    pallas_call x1, Pallas kernels, local(): pl.pallas_call(functools.partial(kernel, n, scale, rows, reach), out_shap...  102 us
    unnamed x1, local copies, waits for them, and re-layouts  2.26 us

profile of v2, /device:TPU:0, one launch (start us, length us, event | category | flops | bytes accessed | tf_op | source)
XLA Modules:
  0.0 104.6 jit_solution(14830683366234602816)
XLA Ops:
  0.0 102.3 %shard_map.82 = f32[4,16,32,128]{3,2,1,0:T(8,128)} custom-call(s32[2,4]{1,0:T(2,128)} %positions.1, f32[2,4]{1,0:T(2,128)} %wavelet.1, f32[2,4,16]{2,1,0:T(4,128)} %traces.1, f32[2,16,64,128]{3,2,1,0:T(8,128)} %src_now.1, f32[2,16,64,128]{3,2,1,0:T(8,128)} %src_prev.1, f32[2,16,64,128]{3,2,1,0:T(8,128)} %rec_now.1, f32[2,16,64,128]{3,2,1,0:T(8,128)} %rec_prev.1, ...), custom_call_target="tpu_custom_call" | custom-call | tf_op jit(solution)/shard_map/pallas_call | solution.py:465
  102.3 2.3 %copy.10 = f32[4,16,32,128]{3,2,1,0:T(8,128)} copy(f32[4,16,32,128]{3,2,1,0:T(8,128)} %shard_map.82) | data formatting | bytes 2097152

commit v3 on v2

--- a/solution.py
+++ b/solution.py
@@ -268,8 +268,8 @@
             pair_copy(g, part).start()
             (send_outer if part else send_inner)(g, y)
 
-    def relay(g):
-        for part in order(g):
+    def relay(g, parts):
+        for part in parts:
             pair_copy(g, part).wait_recv()
             (send_outer if part else send_inner)(g, 1 - y)
 
@@ -379,17 +379,23 @@
     own_out(0)
     wave_step(2)
     send_halo(3)
-    relay(0)
+    relay(0, order(0))
     wave_step(3)
     own_out(1)
     wait_window(0)
     near, far = range(block + 1), range(2 * block + 1, HALF + 1)
 
-    @pl.loop(0, 4)
+    @pl.loop(0, 2)
     def _(chunk):
         image_chunk(0, chunk, range(HALF + 1))
 
-    relay(1)
+    relay(1, (1,))
+
+    @pl.loop(2, 4)
+    def _(chunk):
+        image_chunk(0, chunk, range(HALF + 1))
+
+    relay(1, (0,))
     chunks = [c + y * (3 - 2 * c) for c in range(4)]
     wait_block(1, False, 0)
     wait_block(1, False, 1)

time: 105 us -> 96.2 us (0.916)
  Pallas kernels: 102 us -> 93.7 us
    pallas_call x1, Pallas kernels: 102 us -> 93.7 us  [local(): pl.pallas_call(functools.partial(kernel, n, scale, rows, reach), out_shap...]
where the time goes in v3:
time: 96.2 us; the launch traced here: 96 us
  Pallas kernels  93.7 us (97%)
  local copies, waits for them, and re-layouts  2.26 us (2%)
    pallas_call x1, Pallas kernels, local(): pl.pallas_call(functools.partial(kernel, n, scale, rows, reach), out_shap...  93.7 us
    unnamed x1, local copies, waits for them, and re-layouts  2.26 us

profile of v3, /device:TPU:0, one launch (start us, length us, event | category | flops | bytes accessed | tf_op | source)
XLA Modules:
  0.0 96.0 jit_solution(1000275394150066646)
XLA Ops:
  0.0 93.7 %shard_map.82 = f32[4,16,32,128]{3,2,1,0:T(8,128)} custom-call(s32[2,4]{1,0:T(2,128)} %positions.1, f32[2,4]{1,0:T(2,128)} %wavelet.1, f32[2,4,16]{2,1,0:T(4,128)} %traces.1, f32[2,16,64,128]{3,2,1,0:T(8,128)} %src_now.1, f32[2,16,64,128]{3,2,1,0:T(8,128)} %src_prev.1, f32[2,16,64,128]{3,2,1,0:T(8,128)} %rec_now.1, f32[2,16,64,128]{3,2,1,0:T(8,128)} %rec_prev.1, ...), custom_call_target="tpu_custom_call" | custom-call | tf_op jit(solution)/shard_map/pallas_call | solution.py:471
  93.7 2.3 %copy.10 = f32[4,16,32,128]{3,2,1,0:T(8,128)} copy(f32[4,16,32,128]{3,2,1,0:T(8,128)} %shard_map.82) | data formatting | bytes 2097152
